TPU v7x, 32 devices: a whole 2x2x4 slice. The times are simulated.
32 devices in a mesh: seq: 8 (over z, y), head: 4 (over x, core).
Axes of the slice: x: 2, y: 2, z: 4, core: 2. Of those that a mesh axis runs over, the one named last changes fastest.
Arguments:
- tokens: bfloat16 [2048, 1024], P('seq'), may hold values from -6 to 6
- w_qkv: bfloat16 [1024, 3, 1024], P('seq', None, 'head'), may hold values from -0.1875 to 0.1875
- w_out: bfloat16 [1024, 1024], P('head', 'seq'), may hold values from -1 to 1
- ln1_gain: bfloat16 [1024], P('seq'), may hold values from 0.5 to 1.5
- ln1_bias: bfloat16 [1024], P('seq'), may hold values from -1.796875 to 1.796875
- ln2_gain: bfloat16 [1024], P('seq'), may hold values from 0.5 to 1.5
- ln2_bias: bfloat16 [1024], P('seq'), may hold values from -1.796875 to 1.796875
- w_up: bfloat16 [1024, 4096], P('seq', 'head'), may hold values from -0.1875 to 0.1875
- up_bias: bfloat16 [4096], P('head'), may hold values from -1.796875 to 1.796875
- w_down: bfloat16 [4096, 1024], P('head', 'seq'), may hold values from -0.09375 to 0.09375
- down_bias: bfloat16 [1024], P('seq'), may hold values from -1.796875 to 1.796875
- seq_units: int32 [4], replicated, may hold values from 1 to 4, 8 in all
- seq_pad: int32 [4], replicated, may hold values from 0 to 127
- rand_picks: int32 [32, 16, 3], P('seq', 'head'), may hold values from 0 to 65535
- cotangent: bfloat16 [2048, 1024], P('seq'), may hold values from -6 to 6
Outputs:
- output: bfloat16 [2048, 1024], P('seq')
- x_grad: float32 [2048, 1024], P('seq')
- w_qkv_grad: float32 [1024, 3, 1024], P('seq', None, 'head')
- w_out_grad: float32 [1024, 1024], P('head', 'seq')
- ln1_gain_grad: float32 [1024], P('seq')
- ln1_bias_grad: float32 [1024], P('seq')
- ln2_gain_grad: float32 [1024], P('seq')
- ln2_bias_grad: float32 [1024], P('seq')
- w_up_grad: float32 [1024, 4096], P('seq', 'head')
- up_bias_grad: float32 [4096], P('head')
- w_down_grad: float32 [4096, 1024], P('head', 'seq')
- down_bias_grad: float32 [1024], P('seq')
Inputs may be any that keep to these rules, and one draw needn't show every extreme that they name: `seq_units`: each sequence covers whole units; the values add up to the number of units in the stream, and some sequence covers 4 units.
All inputs are finite; a program needn't handle non-finite values.
Results may differ from a plain program's by a relative error of at most 0.012.
Values may be sent and summed in bfloat16 or wider, within the bound.
A program may use at most 128 MiB of HBM per device.

v0:
```python
import jax
import jax.numpy as jnp
from jax import lax
from jax.sharding import PartitionSpec as P

HEAD_DIM = 64
BLK = 64
SPAN = 4
BLK_DEV = 4
EPSILON = 1e-05
NEGATIVE = -1e30
F32 = jnp.float32
BF16 = jnp.bfloat16


def shifted(value, axis, steps):
    count = lax.axis_size(axis)
    first, last = (max(0, -steps), min(count, count - steps))
    return lax.ppermute(value, axis, [(i, i + steps) for i in range(first, last)])


def norm_parts(features):
    average = jnp.mean(features, axis=-1, keepdims=True)
    centred = features - average
    spread = jnp.mean(centred * centred, axis=-1, keepdims=True)
    inverse = lax.rsqrt(spread + EPSILON)
    return (centred * inverse, inverse)


def norm_backward(xhat, inverse, scaled):
    first = jnp.mean(scaled, axis=-1, keepdims=True)
    second = jnp.mean(scaled * xhat, axis=-1, keepdims=True)
    return inverse * (scaled - first - xhat * second)


def dot(a, b, dims):
    return lax.dot_general(a, b, (dims, ((), ())), preferred_element_type=F32)


def sequence_place(seq_units, seq_pad):
    device = lax.axis_index("seq")
    start, leader, span, pad = (0, 0, 0, 0)
    for k in range(seq_units.shape[0]):
        units = seq_units[k]
        inside = (device >= start) & (device < start + units)
        leader = jnp.where(inside, start, leader)
        span = jnp.where(inside, units, span)
        pad = jnp.where(inside, seq_pad[k], pad)
        start = start + units
    return (device - leader, span, pad)


def key_counts(position, span, picks):
    blocks = lax.broadcasted_iota(jnp.int32, (1, 1, SPAN * BLK_DEV), 2)
    query = position * BLK_DEV + lax.broadcasted_iota(jnp.int32, (BLK_DEV, 1, 1), 0)
    total = span * BLK_DEV
    count = jnp.zeros((BLK_DEV, picks.shape[1], SPAN * BLK_DEV), F32)
    for wanted in (query - 1, query, query + 1, 0, total - 1):
        count = count + (blocks == wanted).astype(F32)
    chosen = picks % total
    for r in range(picks.shape[2]):
        count = count + (blocks == chosen[:, :, r : r + 1]).astype(F32)
    return jnp.where((query == 0) | (query == total - 1), 1.0, count)


def local_general(
    tokens,
    w_qkv,
    w_out,
    ln1_gain,
    ln1_bias,
    ln2_gain,
    ln2_bias,
    w_up,
    up_bias,
    w_down,
    down_bias,
    seq_units,
    seq_pad,
    rand_picks,
    cotangent,
):
    tok, width = tokens.shape
    heads = w_qkv.shape[2] // HEAD_DIM
    rows = lambda v: lax.all_gather(v, "seq", axis=0, tiled=True)
    cols = lambda v: lax.all_gather(v, "seq", axis=1, tiled=True)
    vectors = jnp.stack([ln1_gain, ln1_bias, ln2_gain, ln2_bias, down_bias], axis=0)
    gain_one, shift_one, gain_two, shift_two, down_shift = [
        v[None].astype(F32) for v in cols(vectors)
    ]
    qkv = rows(w_qkv)
    out_w, up_w, down_w = (cols(w_out), rows(w_up), cols(w_down))
    position, span, pad = sequence_place(seq_units, seq_pad)
    root = SPAN - 1 - position
    inputs = tokens.astype(F32)
    xhat_one, inv_one = norm_parts(inputs)
    normed = (xhat_one * gain_one + shift_one).astype(BF16)
    triple = jnp.einsum("td,dcf->tcf", normed, qkv, preferred_element_type=F32).astype(BF16)
    own = jnp.stack([triple[:, 1], triple[:, 2]], axis=0)
    pieces = [own if o == 0 else shifted(own, "seq", -o) for o in range(1 - SPAN, SPAN)]
    nearby = jnp.stack(pieces, axis=0)
    window = lax.dynamic_slice_in_dim(nearby, root, SPAN, 0)
    split = lambda v: v.reshape(v.shape[0], heads, HEAD_DIM)
    keys = split(window[:, 0].reshape(SPAN * tok, -1))
    values = split(window[:, 1].reshape(SPAN * tok, -1))
    queries = split(triple[:, 0])
    scaling = HEAD_DIM ** (-0.5)
    live = jnp.arange(SPAN * tok, dtype=jnp.int32) < span * tok - pad
    count = jnp.repeat(key_counts(position, span, rand_picks), BLK, axis=2)
    count = jnp.where(live[None, None], count, 0.0)
    count = jnp.transpose(jnp.repeat(count, BLK, axis=0), (1, 0, 2))
    logits = jnp.einsum("qhd,khd->hqk", queries, keys, preferred_element_type=F32) * scaling
    logits = jnp.where(count > 0, logits, NEGATIVE)
    grown = jnp.exp(logits - jnp.max(logits, axis=-1, keepdims=True)) * count
    chances = grown / jnp.sum(grown, axis=-1, keepdims=True)
    chances_low = chances.astype(BF16)
    attended = jnp.einsum("hqk,khd->qhd", chances_low, values, preferred_element_type=F32)
    attended = attended.astype(BF16).reshape(tok, heads * HEAD_DIM)
    middle = inputs + lax.psum(dot(attended, out_w, ((1,), (0,))), "head")
    xhat_two, inv_two = norm_parts(middle)
    normed_two = (xhat_two * gain_two + shift_two).astype(BF16)
    pre_act = dot(normed_two, up_w, ((1,), (0,))) + up_bias.astype(F32)[None]
    hidden, pull = jax.vjp(lambda v: jax.nn.gelu(v, approximate=True), pre_act)
    hidden = hidden.astype(BF16)
    ffn = lax.psum(dot(hidden, down_w, ((1,), (0,))).astype(BF16), "head").astype(F32)
    output = (middle + ffn + down_shift).astype(BF16)
    grad_out = cotangent.astype(F32)
    grad_w_down = dot(hidden, cotangent, ((0,), (0,)))
    grad_pre = pull(dot(cotangent, down_w, ((1,), (1,))))[0].astype(BF16)
    grad_w_up = dot(normed_two, grad_pre, ((0,), (0,)))
    grad_up_bias = lax.psum(jnp.sum(grad_pre.astype(F32), axis=0), "seq")
    grad_two = lax.psum(dot(grad_pre, up_w, ((1,), (1,))), "head")
    grad_middle = grad_out + norm_backward(xhat_two, inv_two, grad_two * gain_two)
    grad_branch = grad_middle.astype(BF16)
    grad_w_out = dot(attended, grad_branch, ((0,), (0,)))
    grad_att = split(dot(grad_branch, out_w, ((1,), (1,))).astype(BF16))
    grad_prob = jnp.einsum("qhd,khd->hqk", grad_att, values, preferred_element_type=F32)
    inner = jnp.sum(chances * grad_prob, axis=-1, keepdims=True)
    grad_logit = (chances * (grad_prob - inner)).astype(BF16)
    dq = scaling * jnp.einsum("hqk,khd->qhd", grad_logit, keys, preferred_element_type=F32)
    dk = scaling * jnp.einsum("hqk,qhd->khd", grad_logit, queries, preferred_element_type=F32)
    dv = jnp.einsum("hqk,qhd->khd", chances_low, grad_att, preferred_element_type=F32)
    part = jnp.stack([dk.reshape(SPAN, tok, -1), dv.reshape(SPAN, tok, -1)], axis=1)
    near = jnp.zeros((2 * SPAN - 1,) + part.shape[1:], F32)
    near = lax.dynamic_update_slice_in_dim(near, part, root, 0)
    owned = near[SPAN - 1]
    for offset in range(1 - SPAN, SPAN):
        if offset:
            owned = owned + shifted(near[offset + SPAN - 1], "seq", offset)
    owned = owned.astype(BF16)
    grad_triple = jnp.stack([dq.reshape(tok, -1).astype(BF16), owned[0], owned[1]], axis=1)
    grad_w_qkv = jnp.einsum("td,tcf->dcf", normed, grad_triple, preferred_element_type=F32)
    grad_one = lax.psum(
        jnp.einsum("tcf,dcf->td", grad_triple, qkv, preferred_element_type=F32), "head"
    )
    x_grad = grad_middle + norm_backward(xhat_one, inv_one, grad_one * gain_one)
    sums = jnp.stack(
        [
            jnp.sum(grad_one * xhat_one, axis=0),
            jnp.sum(grad_one, axis=0),
            jnp.sum(grad_two * xhat_two, axis=0),
            jnp.sum(grad_two, axis=0),
            jnp.sum(grad_out, axis=0),
        ],
        axis=0,
    )
    scatter = lambda v, d: lax.psum_scatter(v, "seq", scatter_dimension=d, tiled=True)
    sums = scatter(sums, 1)
    return (
        output,
        x_grad,
        scatter(grad_w_qkv, 0),
        scatter(grad_w_out, 1),
        sums[0],
        sums[1],
        sums[2],
        sums[3],
        scatter(grad_w_up, 0),
        grad_up_bias,
        scatter(grad_w_down, 1),
        sums[4],
    )


IN_SPECS = (
    P("seq", None),
    P("seq", None, "head"),
    P("head", "seq"),
    P("seq"),
    P("seq"),
    P("seq"),
    P("seq"),
    P("seq", "head"),
    P("head"),
    P("head", "seq"),
    P("seq"),
    P(),
    P(),
    P("seq", "head", None),
    P("seq", None),
)
OUT_SPECS = (
    P("seq", None),
    P("seq", None),
    P("seq", None, "head"),
    P("head", "seq"),
    P("seq"),
    P("seq"),
    P("seq"),
    P("seq"),
    P("seq", "head"),
    P("head"),
    P("head", "seq"),
    P("seq"),
)


def solution(mesh):
    return jax.shard_map(
        local_general, mesh=mesh, in_specs=IN_SPECS, out_specs=OUT_SPECS, check_vma=False
    )
```

profile of v0, /device:TPU:0, one launch (start us, length us, event | category | flops | bytes accessed | tf_op | source)
XLA Modules:
  0.0 851.5 jit_solution(9352380124314227854)
XLA Ops:
  23.5 27.9 %all_gather.15 = bf16[5,1024]{1,0:T(8,128)(2,1)S(1)} all-gather(bf16[5,128]{1,0:T(8,128)(2,1)S(1)} %stack.75), channel_id=1, replica_groups=mesh['seq'=8,'head'=4] {'seq'}, dimensions={1}, use_global_device_ids=true | all-gather | bytes 11520 | tf_op jit(solution)/shard_map/all_gather | solution.py:86
  54.2 27.8 %all_gather.17 = bf16[256,1024]{1,0:T(8,128)(2,1)S(1)} all-gather(bf16[256,128]{1,0:T(8,128)(2,1)} %param.17), channel_id=1, replica_groups=mesh['seq'=8,'head'=4] {'seq'}, dimensions={1}, use_global_device_ids=true | all-gather | bytes 589824 | tf_op jit(solution)/shard_map/all_gather | solution.py:86
  86.1 5.1 collective-permute-start.1
  96.8 4.2 collective-permute-done.3
  101.0 6.9 collective-permute-done.4
  119.3 38.9 %all-reduce.5.cloned.1.call-done = f32[256,1024]{1,0:T(8,128)} async-done(((f32[256,1024]{1,0:T(8,128)}), f32[256,1024]{1,0:T(8,128)}) %all-reduce.5.cloned.1.call-update) | async-done | bytes 1048592 | tf_op jit(solution)/shard_map/psum | solution.py:119
  159.9 52.1 %all-gather.8.cloned.1.call-done = bf16[1024,1024]{1,0:T(8,128)(2,1)} async-done(((bf16[1024,128]{1,0:T(8,128)(2,1)}), bf16[1024,1024]{1,0:T(8,128)(2,1)}) %all-gather.8.cloned.1.call-update) | async-done | bytes 2097168 | tf_op jit(solution)/shard_map/all_gather | solution.py:86
  215.2 46.4 %all-gather.6.cloned.1.call-done = bf16[1024,1024]{1,0:T(8,128)(2,1)} async-done(((bf16[128,1024]{1,0:T(8,128)(2,1)}), bf16[1024,1024]{1,0:T(8,128)(2,1)}) %all-gather.6.cloned.1.call-update) | async-done | bytes 2097168 | tf_op jit(solution)/shard_map/all_gather | solution.py:85
  261.6 3.5 convert_reduce_fusion.2
  271.2 31.2 %all-reduce.9.cloned.1.call-done = f32[256,1024]{1,0:T(8,128)} async-done(((f32[256,1024]{1,0:T(8,128)}), f32[256,1024]{1,0:T(8,128)}) %all-reduce.9.cloned.1.call-update) | async-done | bytes 1048592 | tf_op jit(solution)/shard_map/psum | solution.py:132
  304.2 34.6 %all-reduce.7.cloned.1.call-done = bf16[256,1024]{1,0:T(8,128)(2,1)} async-done(((bf16[256,1024]{1,0:T(8,128)(2,1)}), bf16[256,1024]{1,0:T(8,128)(2,1)}) %all-reduce.7.cloned.1.call-update) | async-done | bytes 524304 | tf_op jit(solution)/shard_map/psum | solution.py:125
  363.6 4.2 collective-permute-start.10
  367.8 4.3 collective-permute-start.11
  379.3 4.2 collective-permute-start.9
  384.4 11.5 %collective-permute-done.11 = f32[2,256,256]{2,1,0:T(8,128)} collective-permute-done((f32[2,256,256]{2,1,0:T(8,128)}, f32[2,256,256]{2,1,0:T(8,128)}, u32[]{:S(2)}, u32[]{:S(2)}) %collective-permute-start.11) | collective-permute-done | bytes 524320 | tf_op jit(solution)/shard_map/ppermute | solution.py:19
  395.9 5.4 collective-permute-done.7
  401.3 10.7 %collective-permute-done.9 = f32[2,256,256]{2,1,0:T(8,128)} collective-permute-done((f32[2,256,256]{2,1,0:T(8,128)}, f32[2,256,256]{2,1,0:T(8,128)}, u32[]{:S(2)}, u32[]{:S(2)}) %collective-permute-start.9) | collective-permute-done | bytes 524320 | tf_op jit(solution)/shard_map/ppermute | solution.py:19
  415.9 41.7 %all-reduce.11.cloned.1.call-done = f32[256,1024]{1,0:T(8,128)} async-done(((f32[256,1024]{1,0:T(8,128)}), f32[256,1024]{1,0:T(8,128)}) %all-reduce.11.cloned.1.call-update) | async-done | bytes 1048592 | tf_op jit(solution)/shard_map/psum | solution.py:153
  472.1 22.1 %psum.39 = f32[1024]{0:T(1024)} all-reduce(f32[1024]{0:T(1024)S(1)} %get-tuple-element.20), channel_id=1, replica_groups=mesh['seq'=8,'head'=4] {'seq'}, use_global_device_ids=true, to_apply=%region_25.26 | all-reduce | flops 1024 | bytes 8192 | tf_op jit(solution)/shard_map/psum | solution.py:131
  495.5 19.4 %reduce-scatter.10.cloned.1.call-done = f32[5,128]{1,0:T(8,128)} async-done(((f32[5,1024]{1,0:T(8,128)}), f32[5,128]{1,0:T(8,128)}) %reduce-scatter.10.cloned.1.call-update) | async-done | bytes 2576 | tf_op jit(solution)/shard_map/reduce_scatter | solution.py:167
  516.3 65.9 %reduce-scatter.8.cloned.1.call-done = f32[256,128]{1,0:T(8,128)} async-done(((f32[256,1024]{1,0:T(8,128)}), f32[256,128]{1,0:T(8,128)}) %reduce-scatter.8.cloned.1.call-update) | async-done | bytes 131088 | tf_op jit(solution)/shard_map/reduce_scatter | solution.py:167
  582.2 78.2 %reduce-scatter.6.cloned.1.call-done = f32[128,3,256]{2,0,1:T(8,128)} async-done(((f32[1024,3,256]{2,0,1:T(8,128)}), f32[128,3,256]{2,0,1:T(8,128)}) %reduce-scatter.6.cloned.1.call-update) | async-done | bytes 393232 | tf_op jit(solution)/shard_map/reduce_scatter | solution.py:167
  660.4 91.4 %reduce-scatter.12.cloned.1.call-done = f32[128,1024]{1,0:T(8,128)} async-done(((f32[1024,1024]{1,0:T(8,128)}), f32[128,1024]{1,0:T(8,128)}) %reduce-scatter.12.cloned.1.call-update) | async-done | bytes 524304 | tf_op jit(solution)/shard_map/reduce_scatter | solution.py:167
  751.8 92.8 %reduce-scatter.14.cloned.1.call-done = f32[1024,128]{1,0:T(8,128)} async-done(((f32[1024,1024]{1,0:T(8,128)}), f32[1024,128]{1,0:T(8,128)}) %reduce-scatter.14.cloned.1.call-update) | async-done | bytes 524304 | tf_op jit(solution)/shard_map/reduce_scatter | solution.py:167
  (164 shorter events, 96.5 us)
Async XLA Ops:
  7.2 74.8 %all-gather.4.cloned.1.call-start = ((), (), s32[]{:S(2)}) async-start(), calls=%async_computation.5 | async-start | bytes 1769472 | tf_op jit(solution)/shard_map/all_gather | solution.py:85
  9.0 149.2 %all-reduce.5.cloned.1.call-start = ((), (), s32[]{:S(2)}) async-start(), calls=%async_computation.6 | async-start | bytes 2097152 | tf_op jit(solution)/shard_map/psum | solution.py:119
  84.2 11.1 %collective-permute-start = (bf16[2,256,256]{1,2,0:T(8,128)(2,1)S(1)}, bf16[2,256,256]{1,2,0:T(8,128)(2,1)S(1)}, u32[]{:S(2)}, u32[]{:S(2)}) collective-permute-start(bf16[2,256,256]{1,2,0:T(8,128)(2,1)S(1)} %pad_maximum_fusion.1), channel_id=1, source_target_pairs={{0,12},{4,16},{8,20},{12,24},{16,28},{1,13},{5,17},{9,21},{13,25},... | collective-permute-start | bytes 786440 | tf_op jit(solution)/shard_map/ppermute | solution.py:19
  86.1 10.6 %collective-permute-start.1 = (bf16[2,256,256]{1,2,0:T(8,128)(2,1)S(1)}, bf16[2,256,256]{1,2,0:T(8,128)(2,1)S(1)}, u32[]{:S(2)}, u32[]{:S(2)}) collective-permute-start(bf16[2,256,256]{1,2,0:T(8,128)(2,1)S(1)} %pad_maximum_fusion.1), channel_id=1, source_target_pairs={{0,8},{4,12},{8,16},{12,20},{16,24},{20,28},{1,9},{5,13},{9,17},{1... | collective-permute-start | bytes 786440 | tf_op jit(solution)/shard_map/ppermute | solution.py:19
  91.3 5.4 collective-permute-start.2
  92.7 8.3 collective-permute-start.3
  94.0 13.9 %collective-permute-start.4 = (bf16[2,256,256]{1,2,0:T(8,128)(2,1)S(1)}, bf16[2,256,256]{1,2,0:T(8,128)(2,1)S(1)}, u32[]{:S(2)}, u32[]{:S(2)}) collective-permute-start(bf16[2,256,256]{1,2,0:T(8,128)(2,1)S(1)} %pad_maximum_fusion.1), channel_id=1, source_target_pairs={{8,0},{12,4},{16,8},{20,12},{24,16},{28,20},{9,1},{13,5},{17,9},{2... | collective-permute-start | bytes 786440 | tf_op jit(solution)/shard_map/ppermute | solution.py:19
  95.3 12.6 %collective-permute-start.5 = (bf16[2,256,256]{1,2,0:T(8,128)(2,1)S(1)}, bf16[2,256,256]{1,2,0:T(8,128)(2,1)S(1)}, u32[]{:S(2)}, u32[]{:S(2)}) collective-permute-start(bf16[2,256,256]{1,2,0:T(8,128)(2,1)S(1)} %pad_maximum_fusion.1), channel_id=1, source_target_pairs={{12,0},{16,4},{20,8},{24,12},{28,16},{13,1},{17,5},{21,9},{25,13},... | collective-permute-start | bytes 786440 | tf_op jit(solution)/shard_map/ppermute | solution.py:19
  117.9 94.0 %all-gather.8.cloned.1.call-start = ((), (), s32[]{:S(2)}) async-start(), calls=%async_computation.8 | async-start | bytes 2359296 | tf_op jit(solution)/shard_map/all_gather | solution.py:86
  118.6 143.0 %all-gather.6.cloned.1.call-start = ((), (), s32[]{:S(2)}) async-start(), calls=%async_computation.7 | async-start | bytes 2359296 | tf_op jit(solution)/shard_map/all_gather | solution.py:85
  119.2 183.2 %all-reduce.9.cloned.1.call-start = ((), (), s32[]{:S(2)}) async-start(), calls=%async_computation.10 | async-start | bytes 2097152 | tf_op jit(solution)/shard_map/psum | solution.py:132
  267.7 71.1 %all-reduce.7.cloned.1.call-start = ((), (), s32[]{:S(2)}) async-start(), calls=%async_computation.9 | async-start | bytes 1048576 | tf_op jit(solution)/shard_map/psum | solution.py:125
  271.0 186.6 %all-reduce.11.cloned.1.call-start = ((), (), s32[]{:S(2)}) async-start(), calls=%async_computation.11 | async-start | bytes 2097152 | tf_op jit(solution)/shard_map/psum | solution.py:153
  363.6 15.7 %collective-permute-start.10 = (f32[2,256,256]{2,1,0:T(8,128)S(1)}, f32[2,256,256]{2,1,0:T(8,128)}, u32[]{:S(2)}, u32[]{:S(2)}) collective-permute-start(f32[2,256,256]{2,1,0:T(8,128)S(1)} %get-tuple-element.26), channel_id=1, source_target_pairs={{0,8},{4,12},{8,16},{12,20},{16,24},{20,28},{1,9},{5,13},{9,17},{1... | collective-permute-start | bytes 1572872 | tf_op jit(solution)/shard_map/ppermute | solution.py:19
  367.8 28.1 %collective-permute-start.11 = (f32[2,256,256]{2,1,0:T(8,128)}, f32[2,256,256]{2,1,0:T(8,128)}, u32[]{:S(2)}, u32[]{:S(2)}) collective-permute-start(f32[2,256,256]{2,1,0:T(8,128)} %get-tuple-element.25), channel_id=1, source_target_pairs={{0,12},{4,16},{8,20},{12,24},{16,28},{1,13},{5,17},{9,21},{13,25},... | collective-permute-start | bytes 1572872 | tf_op jit(solution)/shard_map/ppermute | solution.py:19
  372.1 23.9 %collective-permute-start.6 = (f32[2,256,256]{2,1,0:T(8,128)}, f32[2,256,256]{2,1,0:T(8,128)}, u32[]{:S(2)}, u32[]{:S(2)}) collective-permute-start(f32[2,256,256]{2,1,0:T(8,128)} %get-tuple-element.24), channel_id=1, source_target_pairs={{12,0},{16,4},{20,8},{24,12},{28,16},{13,1},{17,5},{21,9},{25,13},... | collective-permute-start | bytes 1572872 | tf_op jit(solution)/shard_map/ppermute | solution.py:19
  373.3 28.0 %collective-permute-start.7 = (f32[2,256,256]{2,1,0:T(8,128)}, f32[2,256,256]{2,1,0:T(8,128)}, u32[]{:S(2)}, u32[]{:S(2)}) collective-permute-start(f32[2,256,256]{2,1,0:T(8,128)} %get-tuple-element.29), channel_id=1, source_target_pairs={{8,0},{12,4},{16,8},{20,12},{24,16},{28,20},{9,1},{13,5},{17,9},{2... | collective-permute-start | bytes 1572872 | tf_op jit(solution)/shard_map/ppermute | solution.py:19
  374.6 26.7 %collective-permute-start.8 = (f32[2,256,256]{2,1,0:T(8,128)}, f32[2,256,256]{2,1,0:T(8,128)}, u32[]{:S(2)}, u32[]{:S(2)}) collective-permute-start(f32[2,256,256]{2,1,0:T(8,128)} %get-tuple-element.28), channel_id=1, source_target_pairs={{4,0},{8,4},{12,8},{16,12},{20,16},{24,20},{28,24},{5,1},{9,5},{13... | collective-permute-start | bytes 1572872 | tf_op jit(solution)/shard_map/ppermute | solution.py:19
  379.3 32.7 %collective-permute-start.9 = (f32[2,256,256]{2,1,0:T(8,128)}, f32[2,256,256]{2,1,0:T(8,128)}, u32[]{:S(2)}, u32[]{:S(2)}) collective-permute-start(f32[2,256,256]{2,1,0:T(8,128)} %get-tuple-element.27), channel_id=1, source_target_pairs={{0,4},{4,8},{8,12},{12,16},{16,20},{20,24},{24,28},{1,5},{5,9},{9,... | collective-permute-start | bytes 1572872 | tf_op jit(solution)/shard_map/ppermute | solution.py:19
  415.9 99.1 %reduce-scatter.10.cloned.1.call-start = ((), (), s32[]{:S(2)}) async-start(), calls=%async_computation.14 | async-start | bytes 36864 | tf_op jit(solution)/shard_map/reduce_scatter | solution.py:167
  460.0 122.2 %reduce-scatter.8.cloned.1.call-start = ((), (), s32[]{:S(2)}) async-start(), calls=%async_computation.13 | async-start | bytes 1179648 | tf_op jit(solution)/shard_map/reduce_scatter | solution.py:167
  461.4 199.0 %reduce-scatter.6.cloned.1.call-start = ((), (), s32[]{:S(2)}) async-start(), calls=%async_computation.12 | async-start | bytes 3538944 | tf_op jit(solution)/shard_map/reduce_scatter | solution.py:167
  464.0 287.9 %reduce-scatter.12.cloned.1.call-start = ((), (), s32[]{:S(2)}) async-start(), calls=%async_computation.15 | async-start | bytes 4718592 | tf_op jit(solution)/shard_map/reduce_scatter | solution.py:167
  467.8 376.8 %reduce-scatter.14.cloned.1.call-start = ((), (), s32[]{:S(2)}) async-start(), calls=%async_computation.16 | async-start | bytes 4718592 | tf_op jit(solution)/shard_map/reduce_scatter | solution.py:167
  (21 other events, 298.2 us)
Sparse Core Ops, SparseCore 0:
  10.6 48.0 all-gather.3
  118.0 40.1 all-reduce.4
  160.5 51.4 all-gather.7
  214.1 47.4 all-gather.5
  267.8 34.5 all-reduce.8
  305.2 33.5 all-reduce.6
  416.0 41.5 all-reduce.10
  461.0 53.8 reduce-scatter.9
  519.3 62.8 reduce-scatter.7
  586.3 74.0 reduce-scatter.5
  664.6 87.1 reduce-scatter.11
  756.3 88.2 reduce-scatter.13
where the time goes:
time: 853 us; the launch traced here: 851 us
  waiting for transfers between devices  636 us (75%)
  blocking collectives  77.8 us (9%)
  matrix products  35.6 us (4%)
  starting transfers between devices  29.3 us (3%)
  local copies, waits for them, and re-layouts  29.2 us (3%)
  between operations  24.6 us (3%)
  other arithmetic  18.9 us (2%)
    reduce_scatter x5, waiting for transfers between devices, local_general(): lax.psum_scatter(v, 'seq', scatter_dimension=d, tiled=True)  348 us
    all_gather x2, blocking collectives, local_general(): cols = lambda v: lax.all_gather(v, 'seq', axis=1, tiled=True)  55.7 us
    all_gather x1, waiting for transfers between devices, local_general(): cols = lambda v: lax.all_gather(v, 'seq', axis=1, tiled=True)  52.1 us
    all_gather x2, waiting for transfers between devices, local_general(): rows = lambda v: lax.all_gather(v, 'seq', axis=0, tiled=True)  46.4 us
    ppermute x12, waiting for transfers between devices, shifted(): lax.ppermute(value, axis, [(i, i + steps) for i in range(first, last)])  42.2 us
    psum x1, waiting for transfers between devices, local_general(): lax.psum(jnp.einsum('tcf,dcf->td', grad_triple, qkv, preferred_element_ty...  41.7 us
    psum x1, waiting for transfers between devices, local_general(): middle = inputs + lax.psum(dot(attended, out_w, ((1,), (0,))), 'head')  38.9 us
    psum x1, waiting for transfers between devices, local_general(): lax.psum(dot(hidden, down_w, ((1,), (0,))).astype(BF16), 'head').astype(F32)  34.6 us
  transfers between devices with their start and end apart: 24, of which 17 were waited for; matrix products, arithmetic and copies ran while one was open for 4% of the time, Pallas kernels for 0%

commit v1 on v0

--- a/solution.py
+++ b/solution.py
@@ -11,6 +11,19 @@
 NEGATIVE = -1e30
 F32 = jnp.float32
 BF16 = jnp.bfloat16
+
+
+def gather_around(x, axis, dim):
+    ways = lax.axis_size(axis)
+    up = [(d, (d + 1) % ways) for d in range(ways)]
+    down = [(d, (d - 1) % ways) for d in range(ways)]
+    earlier, later = ([x], [x])
+    for _ in range(ways // 2):
+        earlier.append(lax.ppermute(earlier[-1], axis, up))
+    for _ in range((ways - 1) // 2):
+        later.append(lax.ppermute(later[-1], axis, down))
+    line = jnp.concatenate([*earlier[::-1], *later[1:]], axis=dim)
+    return jnp.roll(line, (lax.axis_index(axis) - ways // 2) * x.shape[dim], axis=dim)
 
 
 def shifted(value, axis, steps):
@@ -82,7 +95,7 @@
 ):
     tok, width = tokens.shape
     heads = w_qkv.shape[2] // HEAD_DIM
-    rows = lambda v: lax.all_gather(v, "seq", axis=0, tiled=True)
+    rows = lambda v: gather_around(v, "seq", 0)
     cols = lambda v: lax.all_gather(v, "seq", axis=1, tiled=True)
     vectors = jnp.stack([ln1_gain, ln1_bias, ln2_gain, ln2_bias, down_bias], axis=0)
     gain_one, shift_one, gain_two, shift_two, down_shift = [

time: 853 us -> 822 us (0.964)
  waiting for transfers between devices: 636 us -> 550 us
  starting transfers between devices: 29.3 us -> 68.5 us
  local copies, waits for them, and re-layouts: 29.2 us -> 42.4 us
    all_gather x1, waiting for transfers between devices: 52.1 us -> 1.25 us  [local_general(): cols = lambda v: lax.all_gather(v, 'seq', axis=1, tiled=True)]
    ppermute x0 -> x14, waiting for transfers between devices: none -> 48.8 us  [the longest x8 47.5 us: gather_around(): earlier.append(lax.ppermute(earlier[-1], axis, up))]
    all_gather x2 -> x0, waiting for transfers between devices: 46.4 us -> none  [local_general(): rows = lambda v: lax.all_gather(v, 'seq', axis=0, tiled=True)]
    psum x1, waiting for transfers between devices: 38.9 us -> 0.01 us  [local_general(): middle = inputs + lax.psum(dot(attended, out_w, ((1,), (0,))), 'head')]
    ppermute x0 -> x14, starting transfers between devices: none -> 36.5 us  [the longest x6 22.6 us: gather_around(): later.append(lax.ppermute(later[-1], axis, down))]
    psum x1, waiting for transfers between devices: 41.7 us -> 55.7 us  [local_general(): lax.psum(jnp.einsum('tcf,dcf->td', grad_triple, qkv, preferred_element_ty...]
    unnamed x48 -> x108, local copies, waits for them, and re-layouts: 9.05 us -> 21.5 us
    ppermute x12, waiting for transfers between devices: 42.2 us -> 33.4 us  [shifted(): lax.ppermute(value, axis, [(i, i + steps) for i in range(first, last)])]
  transfers between devices with their start and end apart: 24 -> 36, of which waited for: 17 -> 24; matrix products, arithmetic and copies ran while one was open for 4% -> 5% of each run, Pallas kernels for 0% -> 0%
where the time goes in v1:
time: 822 us; the launch traced here: 820 us
  waiting for transfers between devices  550 us (67%)
  blocking collectives  76.1 us (9%)
  starting transfers between devices  68.5 us (8%)
  local copies, waits for them, and re-layouts  42.4 us (5%)
  matrix products  36.5 us (4%)
  between operations  26 us (3%)
  other arithmetic  20.6 us (3%)
    reduce_scatter x5, waiting for transfers between devices, local_general(): lax.psum_scatter(v, 'seq', scatter_dimension=d, tiled=True)  345 us
    psum x1, waiting for transfers between devices, local_general(): lax.psum(jnp.einsum('tcf,dcf->td', grad_triple, qkv, preferred_element_ty...  55.7 us
    all_gather x2, blocking collectives, local_general(): cols = lambda v: lax.all_gather(v, 'seq', axis=1, tiled=True)  54.2 us
    ppermute x8, waiting for transfers between devices, gather_around(): earlier.append(lax.ppermute(earlier[-1], axis, up))  47.5 us
    psum x1, waiting for transfers between devices, local_general(): lax.psum(dot(hidden, down_w, ((1,), (0,))).astype(BF16), 'head').astype(F32)  34.2 us
    ppermute x12, waiting for transfers between devices, shifted(): lax.ppermute(value, axis, [(i, i + steps) for i in range(first, last)])  33.4 us
    psum x1, waiting for transfers between devices, local_general(): grad_two = lax.psum(dot(grad_pre, up_w, ((1,), (1,))), 'head')  31.6 us
    ppermute x12, starting transfers between devices, shifted(): lax.ppermute(value, axis, [(i, i + steps) for i in range(first, last)])  31.3 us
  transfers between devices with their start and end apart: 36, of which 24 were waited for; matrix products, arithmetic and copies ran while one was open for 5% of the time, Pallas kernels for 0%

profile of v1, /device:TPU:0, one launch (start us, length us, event | category | flops | bytes accessed | tf_op | source)
XLA Modules:
  0.0 820.2 jit_solution(11644250693280393498)
XLA Ops:
  24.6 26.0 %all_gather.9 = bf16[5,1024]{1,0:T(8,128)(2,1)S(1)} all-gather(bf16[5,128]{1,0:T(8,128)(2,1)S(1)} %stack.75), channel_id=1, replica_groups=mesh['seq'=8,'head'=4] {'seq'}, dimensions={1}, use_global_device_ids=true | all-gather | bytes 11520 | tf_op jit(solution)/shard_map/all_gather | solution.py:99
  56.3 28.2 %all_gather.10 = bf16[256,1024]{1,0:T(8,128)(2,1)S(1)} all-gather(bf16[256,128]{1,0:T(8,128)(2,1)} %param.17), channel_id=1, replica_groups=mesh['seq'=8,'head'=4] {'seq'}, dimensions={1}, use_global_device_ids=true | all-gather | bytes 589824 | tf_op jit(solution)/shard_map/all_gather | solution.py:99
  86.6 8.3 %collective-permute-done.1 = bf16[128,3,256]{0,2,1:T(8,128)(2,1)S(1)} collective-permute-done((bf16[128,3,256]{0,2,1:T(8,128)(2,1)S(1)}, bf16[128,3,256]{0,2,1:T(8,128)(2,1)S(1)}, u32[]{:S(2)}, u32[]{:S(2)}) %collective-permute-start.1) | collective-permute-done | bytes 196640 | tf_op jit(solution)/shard_map/ppermute | solution.py:22
  95.1 4.8 collective-permute-start.5
  103.4 4.9 collective-permute-start.6
  128.9 7.8 collective-permute-done.10
  152.9 5.9 collective-permute-start.13
  158.8 8.7 %collective-permute-done.13 = bf16[128,1024]{1,0:T(8,128)(2,1)S(1)} collective-permute-done((bf16[128,1024]{1,0:T(8,128)(2,1)S(1)}, bf16[128,1024]{1,0:T(8,128)(2,1)S(1)}, u32[]{:S(2)}, u32[]{:S(2)}) %collective-permute-start.13) | collective-permute-done | bytes 262176 | tf_op jit(solution)/shard_map/ppermute | solution.py:22
  172.3 8.6 %collective-permute-done.14 = bf16[128,1024]{1,0:T(8,128)(2,1)S(1)} collective-permute-done((bf16[128,1024]{1,0:T(8,128)(2,1)S(1)}, bf16[128,1024]{1,0:T(8,128)(2,1)S(1)}, u32[]{:S(2)}, u32[]{:S(2)}) %collective-permute-start.14) | collective-permute-done | bytes 262176 | tf_op jit(solution)/shard_map/ppermute | solution.py:22
  186.0 6.8 collective-permute-done.15
  192.8 4.9 collective-permute-start.19
  197.8 8.1 collective-permute-done.16
  233.9 31.6 %all-reduce.9.cloned.1.call-done = f32[256,1024]{1,0:T(8,128)} async-done(((f32[256,1024]{1,0:T(8,128)}), f32[256,1024]{1,0:T(8,128)}) %all-reduce.9.cloned.1.call-update) | async-done | bytes 1048592 | tf_op jit(solution)/shard_map/psum | solution.py:145
  267.8 34.2 %all-reduce.7.cloned.1.call-done = bf16[256,1024]{1,0:T(8,128)(2,1)} async-done(((bf16[256,1024]{1,0:T(8,128)(2,1)}), bf16[256,1024]{1,0:T(8,128)(2,1)}) %all-reduce.7.cloned.1.call-update) | async-done | bytes 524304 | tf_op jit(solution)/shard_map/psum | solution.py:138
  331.3 5.4 collective-permute-start.23
  345.1 6.0 collective-permute-start.25
  355.7 11.6 %collective-permute-done.23 = f32[2,256,256]{2,1,0:T(8,128)} collective-permute-done((f32[2,256,256]{2,1,0:T(8,128)}, f32[2,256,256]{2,1,0:T(8,128)}, u32[]{:S(2)}, u32[]{:S(2)}) %collective-permute-start.23) | collective-permute-done | bytes 524320 | tf_op jit(solution)/shard_map/ppermute | solution.py:32
  371.3 55.7 %all-reduce.11.cloned.1.call-done = f32[256,1024]{1,0:T(8,128)} async-done(((f32[256,1024]{1,0:T(8,128)}), f32[256,1024]{1,0:T(8,128)}) %all-reduce.11.cloned.1.call-update) | async-done | bytes 1048592 | tf_op jit(solution)/shard_map/psum | solution.py:166
  443.3 21.9 %psum.39 = f32[1024]{0:T(1024)} all-reduce(f32[1024]{0:T(1024)S(1)} %copy-done.34), channel_id=1, replica_groups=mesh['seq'=8,'head'=4] {'seq'}, use_global_device_ids=true, to_apply=%region_25.26 | all-reduce | flops 1024 | bytes 8192 | tf_op jit(solution)/shard_map/psum | solution.py:144
  466.6 17.6 %reduce-scatter.10.cloned.1.call-done = f32[5,128]{1,0:T(8,128)} async-done(((f32[5,1024]{1,0:T(8,128)}), f32[5,128]{1,0:T(8,128)}) %reduce-scatter.10.cloned.1.call-update) | async-done | bytes 2576 | tf_op jit(solution)/shard_map/reduce_scatter | solution.py:180
  485.6 66.0 %reduce-scatter.8.cloned.1.call-done = f32[256,128]{1,0:T(8,128)} async-done(((f32[256,1024]{1,0:T(8,128)}), f32[256,128]{1,0:T(8,128)}) %reduce-scatter.8.cloned.1.call-update) | async-done | bytes 131088 | tf_op jit(solution)/shard_map/reduce_scatter | solution.py:180
  551.5 77.8 %reduce-scatter.6.cloned.1.call-done = f32[128,3,256]{2,0,1:T(8,128)} async-done(((f32[1024,3,256]{2,0,1:T(8,128)}), f32[128,3,256]{2,0,1:T(8,128)}) %reduce-scatter.6.cloned.1.call-update) | async-done | bytes 393232 | tf_op jit(solution)/shard_map/reduce_scatter | solution.py:180
  629.4 91.1 %reduce-scatter.12.cloned.1.call-done = f32[128,1024]{1,0:T(8,128)} async-done(((f32[1024,1024]{1,0:T(8,128)}), f32[128,1024]{1,0:T(8,128)}) %reduce-scatter.12.cloned.1.call-update) | async-done | bytes 524304 | tf_op jit(solution)/shard_map/reduce_scatter | solution.py:180
  720.5 92.6 %reduce-scatter.14.cloned.1.call-done = f32[1024,128]{1,0:T(8,128)} async-done(((f32[1024,1024]{1,0:T(8,128)}), f32[1024,128]{1,0:T(8,128)}) %reduce-scatter.14.cloned.1.call-update) | async-done | bytes 524304 | tf_op jit(solution)/shard_map/reduce_scatter | solution.py:180
  (248 shorter events, 159.6 us)
Async XLA Ops:
  8.0 209.4 %all-reduce.5.cloned.1.call-start = ((), (), s32[]{:S(2)}) async-start(), calls=%async_computation.5 | async-start | bytes 2097152 | tf_op jit(solution)/shard_map/psum | solution.py:132
  9.1 77.4 %collective-permute-start = (bf16[128,3,256]{0,2,1:T(8,128)(2,1)S(1)}, bf16[128,3,256]{0,2,1:T(8,128)(2,1)S(1)}, u32[]{:S(2)}, u32[]{:S(2)}) collective-permute-start(bf16[128,3,256]{0,2,1:T(8,128)(2,1)S(1)} %copy.39), channel_id=1, source_target_pairs={{0,4},{4,8},{8,12},{12,16},{16,20},{20,24},{24,28},{28,0},{1,5},{5... | collective-permute-start | bytes 589832 | tf_op jit(solution)/shard_map/ppermute | solution.py:22
  12.2 82.9 %collective-permute-start.4 = (bf16[128,3,256]{0,2,1:T(8,128)(2,1)S(1)}, bf16[128,3,256]{0,2,1:T(8,128)(2,1)S(1)}, u32[]{:S(2)}, u32[]{:S(2)}) collective-permute-start(bf16[128,3,256]{0,2,1:T(8,128)(2,1)S(1)} %copy.39), channel_id=1, source_target_pairs={{0,28},{4,0},{8,4},{12,8},{16,12},{20,16},{24,20},{28,24},{1,29},{... | collective-permute-start | bytes 589832 | tf_op jit(solution)/shard_map/ppermute | solution.py:24
  125.8 15.1 %collective-permute-start.11 = (bf16[2,256,256]{1,2,0:T(8,128)(2,1)S(1)}, bf16[2,256,256]{1,2,0:T(8,128)(2,1)S(1)}, u32[]{:S(2)}, u32[]{:S(2)}) collective-permute-start(bf16[2,256,256]{1,2,0:T(8,128)(2,1)S(1)} %pad_maximum_fusion.1), channel_id=1, source_target_pairs={{8,0},{12,4},{16,8},{20,12},{24,16},{28,20},{9,1},{13,5},{17,9},{2... | collective-permute-start | bytes 786440 | tf_op jit(solution)/shard_map/ppermute | solution.py:32
  127.1 15.7 %collective-permute-start.12 = (bf16[2,256,256]{1,2,0:T(8,128)(2,1)S(1)}, bf16[2,256,256]{1,2,0:T(8,128)(2,1)S(1)}, u32[]{:S(2)}, u32[]{:S(2)}) collective-permute-start(bf16[2,256,256]{1,2,0:T(8,128)(2,1)S(1)} %pad_maximum_fusion.1), channel_id=1, source_target_pairs={{12,0},{16,4},{20,8},{24,12},{28,16},{13,1},{17,5},{21,9},{25,13},... | collective-permute-start | bytes 786440 | tf_op jit(solution)/shard_map/ppermute | solution.py:32
  152.8 67.6 %all-gather.2.cloned.1.call-start = ((), (), s32[]{:S(2)}) async-start(), calls=%async_computation.6 | async-start | bytes 2359296 | tf_op jit(solution)/shard_map/all_gather | solution.py:99
  152.9 14.7 %collective-permute-start.13 = (bf16[128,1024]{1,0:T(8,128)(2,1)S(1)}, bf16[128,1024]{1,0:T(8,128)(2,1)S(1)}, u32[]{:S(2)}, u32[]{:S(2)}) collective-permute-start(bf16[128,1024]{1,0:T(8,128)(2,1)S(1)} %copy-done.14), channel_id=1, source_target_pairs={{0,4},{4,8},{8,12},{12,16},{16,20},{20,24},{24,28},{28,0},{1,5},{5... | collective-permute-start | bytes 786440 | tf_op jit(solution)/shard_map/ppermute | solution.py:22
  158.8 106.7 %all-reduce.9.cloned.1.call-start = ((), (), s32[]{:S(2)}) async-start(), calls=%async_computation.8 | async-start | bytes 2097152 | tf_op jit(solution)/shard_map/psum | solution.py:145
  167.6 13.4 %collective-permute-start.14 = (bf16[128,1024]{1,0:T(8,128)(2,1)S(1)}, bf16[128,1024]{1,0:T(8,128)(2,1)S(1)}, u32[]{:S(2)}, u32[]{:S(2)}) collective-permute-start(bf16[128,1024]{1,0:T(8,128)(2,1)S(1)} %collective-permute-done.13), channel_id=1, source_target_pairs={{0,4},{4,8},{8,12},{12,16},{16,20},{20,24},{24,28},{28,0},{1,5},{5... | collective-permute-start | bytes 786440 | tf_op jit(solution)/shard_map/ppermute | solution.py:22
  170.0 13.4 %collective-permute-start.17 = (bf16[128,1024]{1,0:T(8,128)(2,1)S(1)}, bf16[128,1024]{1,0:T(8,128)(2,1)S(1)}, u32[]{:S(2)}, u32[]{:S(2)}) collective-permute-start(bf16[128,1024]{1,0:T(8,128)(2,1)S(1)} %copy-done.14), channel_id=1, source_target_pairs={{0,28},{4,0},{8,4},{12,8},{16,12},{20,16},{24,20},{28,24},{1,29},{... | collective-permute-start | bytes 786440 | tf_op jit(solution)/shard_map/ppermute | solution.py:24
  192.8 18.1 %collective-permute-start.19 = (bf16[128,1024]{1,0:T(8,128)(2,1)S(1)}, bf16[128,1024]{1,0:T(8,128)(2,1)S(1)}, u32[]{:S(2)}, u32[]{:S(2)}) collective-permute-start(bf16[128,1024]{1,0:T(8,128)(2,1)S(1)} %collective-permute-done.18), channel_id=1, source_target_pairs={{0,28},{4,0},{8,4},{12,8},{16,12},{20,16},{24,20},{28,24},{1,29},{... | collective-permute-start | bytes 786440 | tf_op jit(solution)/shard_map/ppermute | solution.py:24
  230.5 71.4 %all-reduce.7.cloned.1.call-start = ((), (), s32[]{:S(2)}) async-start(), calls=%async_computation.7 | async-start | bytes 1048576 | tf_op jit(solution)/shard_map/psum | solution.py:138
  233.8 193.2 %all-reduce.11.cloned.1.call-start = ((), (), s32[]{:S(2)}) async-start(), calls=%async_computation.9 | async-start | bytes 2097152 | tf_op jit(solution)/shard_map/psum | solution.py:166
  327.4 17.7 %collective-permute-start.20 = (f32[2,256,256]{2,1,0:T(8,128)S(1)}, f32[2,256,256]{2,1,0:T(8,128)S(1)}, u32[]{:S(2)}, u32[]{:S(2)}) collective-permute-start(f32[2,256,256]{2,1,0:T(8,128)S(1)} %get-tuple-element.24), channel_id=1, source_target_pairs={{12,0},{16,4},{20,8},{24,12},{28,16},{13,1},{17,5},{21,9},{25,13},... | collective-permute-start | bytes 1572872 | tf_op jit(solution)/shard_map/ppermute | solution.py:32
  328.7 27.0 %collective-permute-start.21 = (f32[2,256,256]{2,1,0:T(8,128)}, f32[2,256,256]{2,1,0:T(8,128)}, u32[]{:S(2)}, u32[]{:S(2)}) collective-permute-start(f32[2,256,256]{2,1,0:T(8,128)} %get-tuple-element.29), channel_id=1, source_target_pairs={{8,0},{12,4},{16,8},{20,12},{24,16},{28,20},{9,1},{13,5},{17,9},{2... | collective-permute-start | bytes 1572872 | tf_op jit(solution)/shard_map/ppermute | solution.py:32
  330.0 25.7 %collective-permute-start.22 = (f32[2,256,256]{2,1,0:T(8,128)}, f32[2,256,256]{2,1,0:T(8,128)}, u32[]{:S(2)}, u32[]{:S(2)}) collective-permute-start(f32[2,256,256]{2,1,0:T(8,128)} %get-tuple-element.28), channel_id=1, source_target_pairs={{4,0},{8,4},{12,8},{16,12},{20,16},{24,20},{28,24},{5,1},{9,5},{13... | collective-permute-start | bytes 1572872 | tf_op jit(solution)/shard_map/ppermute | solution.py:32
  331.3 36.0 %collective-permute-start.23 = (f32[2,256,256]{2,1,0:T(8,128)}, f32[2,256,256]{2,1,0:T(8,128)}, u32[]{:S(2)}, u32[]{:S(2)}) collective-permute-start(f32[2,256,256]{2,1,0:T(8,128)} %get-tuple-element.27), channel_id=1, source_target_pairs={{0,4},{4,8},{8,12},{12,16},{16,20},{20,24},{24,28},{1,5},{5,9},{9,... | collective-permute-start | bytes 1572872 | tf_op jit(solution)/shard_map/ppermute | solution.py:32
  336.7 30.6 %collective-permute-start.24 = (f32[2,256,256]{2,1,0:T(8,128)}, f32[2,256,256]{2,1,0:T(8,128)}, u32[]{:S(2)}, u32[]{:S(2)}) collective-permute-start(f32[2,256,256]{2,1,0:T(8,128)} %get-tuple-element.26), channel_id=1, source_target_pairs={{0,8},{4,12},{8,16},{12,20},{16,24},{20,28},{1,9},{5,13},{9,17},{1... | collective-permute-start | bytes 1572872 | tf_op jit(solution)/shard_map/ppermute | solution.py:32
  345.1 22.2 %collective-permute-start.25 = (f32[2,256,256]{2,1,0:T(8,128)}, f32[2,256,256]{2,1,0:T(8,128)}, u32[]{:S(2)}, u32[]{:S(2)}) collective-permute-start(f32[2,256,256]{2,1,0:T(8,128)} %get-tuple-element.25), channel_id=1, source_target_pairs={{0,12},{4,16},{8,20},{12,24},{16,28},{1,13},{5,17},{9,21},{13,25},... | collective-permute-start | bytes 1572872 | tf_op jit(solution)/shard_map/ppermute | solution.py:32
  371.0 113.1 %reduce-scatter.10.cloned.1.call-start = ((), (), s32[]{:S(2)}) async-start(), calls=%async_computation.12 | async-start | bytes 36864 | tf_op jit(solution)/shard_map/reduce_scatter | solution.py:180
  430.1 121.5 %reduce-scatter.8.cloned.1.call-start = ((), (), s32[]{:S(2)}) async-start(), calls=%async_computation.11 | async-start | bytes 1179648 | tf_op jit(solution)/shard_map/reduce_scatter | solution.py:180
  431.5 197.9 %reduce-scatter.6.cloned.1.call-start = ((), (), s32[]{:S(2)}) async-start(), calls=%async_computation.10 | async-start | bytes 3538944 | tf_op jit(solution)/shard_map/reduce_scatter | solution.py:180
  434.7 285.8 %reduce-scatter.12.cloned.1.call-start = ((), (), s32[]{:S(2)}) async-start(), calls=%async_computation.13 | async-start | bytes 4718592 | tf_op jit(solution)/shard_map/reduce_scatter | solution.py:180
  438.3 374.8 %reduce-scatter.14.cloned.1.call-start = ((), (), s32[]{:S(2)}) async-start(), calls=%async_computation.14 | async-start | bytes 4718592 | tf_op jit(solution)/shard_map/reduce_scatter | solution.py:180
  (48 other events, 939.9 us)
Sparse Core Ops, SparseCore 0:
  152.9 38.7 all-reduce.4
  230.6 34.7 all-reduce.8
  268.4 33.5 all-reduce.6
  371.1 55.8 all-reduce.10
Sparse Core Ops, SparseCore 1:
  158.9 61.5 all-gather.1
  430.1 54.0 reduce-scatter.9
  488.4 63.1 reduce-scatter.7
  555.7 73.6 reduce-scatter.5
  633.6 86.8 reduce-scatter.11
  725.2 87.9 reduce-scatter.13
